TPU v7x, 32 devices: a whole 2x2x4 slice. The times are simulated.
32 devices in a mesh: dp: 8 (over z, x), band: 4 (over y, core).
Axes of the slice: x: 2, y: 2, z: 4, core: 2. Of those that a mesh axis runs over, the one named last changes fastest.
Arguments:
- inputs: bfloat16 [2, 8, 2048, 768], P(None, 'dp', 'band'), may hold values from -6 to 6
- segments: int32 [2, 8, 2048], P(None, 'dp', 'band'), may hold values from 0 to 6, as said below
- cotangent: bfloat16 [2, 8, 2048, 768], P(None, 'dp', 'band'), may hold values from -6 to 6
- ln1_gain: bfloat16 [768], P('band'), may hold values from 0.5 to 1.5
- ln1_bias: bfloat16 [768], P('band'), may hold values from -3 to 3
- w_qkv: bfloat16 [768, 2304], P('band'), may hold values from -0.21875 to 0.21875
- b_qv: bfloat16 [1536], P('band'), may hold values from -0.4375 to 0.4375
- w_out: bfloat16 [768, 768], P('band'), may hold values from -2.5 to 2.5
- b_out: bfloat16 [768], P('band'), may hold values from -3 to 3
- ln2_gain: bfloat16 [768], P('band'), may hold values from 0.5 to 1.5
- ln2_bias: bfloat16 [768], P('band'), may hold values from -3 to 3
- w_up: bfloat16 [768, 3072], P('band'), may hold values from -0.21875 to 0.21875
- b_up: bfloat16 [3072], P('band'), may hold values from -3 to 3
- w_down: bfloat16 [3072, 768], P('band'), may hold values from -0.109375 to 0.109375
- b_down: bfloat16 [768], P('band'), may hold values from -3 to 3
Outputs:
- output: bfloat16 [2, 8, 2048, 768], P(None, 'dp', 'band')
- input_grad: bfloat16 [2, 8, 2048, 768], P(None, 'dp', 'band')
- grad_ln1_gain: float32 [768], P('band')
- grad_ln1_bias: float32 [768], P('band')
- grad_w_qkv: float32 [768, 2304], P('band')
- grad_b_qv: float32 [1536], P('band')
- grad_w_out: float32 [768, 768], P('band')
- grad_b_out: float32 [768], P('band')
- grad_ln2_gain: float32 [768], P('band')
- grad_ln2_bias: float32 [768], P('band')
- grad_w_up: float32 [768, 3072], P('band')
- grad_b_up: float32 [3072], P('band')
- grad_w_down: float32 [3072, 768], P('band')
- grad_b_down: float32 [768], P('band')
Inputs may be any that keep to these rules, and one draw needn't show every extreme that they name: `segments`: each sequence's 2048 slots are consecutive blocks of 512 slots that carry the same ids in the same order. In a block, ids never fall: tiles 1, 2, 3 and so on are contiguous runs, and padding (0) fills the end of the block, at most 51 slots.
All inputs are finite; a program needn't handle non-finite values.
Results may differ from a plain program's by a relative error of at most 0.02.
Values may be sent and summed in bfloat16 or wider, within the bound.
No kernel may reach another device: no remote copies, remote signals or barrier semaphores. Data moves between devices by JAX's collectives and lax.ppermute only.
A program may use at most 192 MiB of HBM per device.

v0:
```python
import jax
import jax.numpy as jnp
from jax import lax
from jax.sharding import PartitionSpec as P

HD = 64
D = 768


def inner_dot(left, right):
    return jnp.dot(left, right, preferred_element_type=jnp.float32)


def row_dot(left, right):
    return lax.dot_general(
        left, right, (((0,), (0,)), ((), ())), preferred_element_type=jnp.float32
    )


def col_dot(left, right):
    return lax.dot_general(
        left, right, (((1,), (1,)), ((), ())), preferred_element_type=jnp.float32
    )


def normed(value, gain, shift):
    center = value - jnp.mean(value, axis=-1, keepdims=True)
    spread = jnp.mean(center * center, axis=-1, keepdims=True)
    return center * lax.rsqrt(spread + 1e-06) * gain + shift


def gelu_tanh(value):
    return jax.nn.gelu(value, approximate=True)


def split_heads(block, heads):
    return block.reshape(block.shape[0], heads, -1).transpose(1, 0, 2)


def merge_heads(block):
    return block.transpose(1, 0, 2).reshape(block.shape[1], -1)


def blocks_of(array, count):
    return array.reshape((count, array.shape[0] // count) + array.shape[1:])


def masked_scores(query, keys, seg_query, seg_keys):
    scores = col_dot(query, keys) * 0.125
    return jnp.where(seg_query[:, None] == seg_keys[None, :], scores, -1e30)


def attend_forward(query, keys, values, seg_query, seg_keys, count):

    def per_head(item):
        head_query, head_keys, head_values = item

        def per_block(piece):
            block_query, block_seg = piece
            scores = masked_scores(block_query, head_keys, block_seg, seg_keys)
            peak = jnp.max(scores, axis=-1, keepdims=True)
            raised = jnp.exp(scores - peak)
            total = jnp.sum(raised, axis=-1, keepdims=True)
            weights = (raised / total).astype(jnp.bfloat16)
            return (inner_dot(weights, head_values), (peak + jnp.log(total))[:, 0])

        result, log_total = lax.map(
            per_block, (blocks_of(head_query, count), blocks_of(seg_query, count))
        )
        return (result.reshape(head_query.shape), log_total.reshape(-1))

    return lax.map(per_head, (query, keys, values))


def attend_backward(query, keys, values, grad_out, log_total, seg_query, seg_keys, count):

    def per_head(item):
        head_query, head_keys, head_values, head_grad, head_total = item

        def per_block(carry, piece):
            grad_keys, grad_values = carry
            block_query, block_grad, block_total, block_seg = piece
            scores = masked_scores(block_query, head_keys, block_seg, seg_keys)
            weights = jnp.exp(scores - block_total[:, None])
            grad_values = grad_values + row_dot(weights.astype(jnp.bfloat16), block_grad)
            grad_weights = col_dot(block_grad, head_values)
            center = jnp.sum(weights * grad_weights, axis=-1, keepdims=True)
            grad_scores = (weights * (grad_weights - center)).astype(jnp.bfloat16)
            grad_query = inner_dot(grad_scores, head_keys) * 0.125
            grad_keys = grad_keys + row_dot(grad_scores, block_query) * 0.125
            return ((grad_keys, grad_values), grad_query)

        start = jnp.zeros(head_keys.shape, jnp.float32)
        (grad_keys, grad_values), grad_query = lax.scan(
            per_block,
            (start, start),
            (
                blocks_of(head_query, count),
                blocks_of(head_grad, count),
                blocks_of(head_total, count),
                blocks_of(seg_query, count),
            ),
        )
        return (grad_query.reshape(head_query.shape), grad_keys, grad_values)

    return lax.map(per_head, (query, keys, values, grad_out, log_total))


def layer_pass(inputs, segment, cotangent, whole, parts):
    (
        gain_one,
        shift_one,
        w_proj,
        b_proj,
        w_mix,
        b_mix,
        gain_two,
        shift_two,
        w_rise,
        b_rise,
        w_fall,
        b_fall,
    ) = whole
    gain_one = gain_one.astype(jnp.float32)
    shift_one = shift_one.astype(jnp.float32)
    gain_two = gain_two.astype(jnp.float32)
    shift_two = shift_two.astype(jnp.float32)
    b_proj = b_proj.astype(jnp.float32)
    b_mix = b_mix.astype(jnp.float32)
    b_rise = b_rise.astype(jnp.float32)
    b_fall = b_fall.astype(jnp.float32)
    heads = D // HD
    count = max(inputs.shape[0] // 512, 1)
    value = inputs.astype(jnp.float32)
    normed_in, pull_one = jax.vjp(normed, value, gain_one, shift_one)
    normed_low = normed_in.astype(jnp.bfloat16)
    projected = inner_dot(normed_low, w_proj)
    query = (projected[:, :D] + b_proj[:D]).astype(jnp.bfloat16)
    key_part = projected[:, D : 2 * D].astype(jnp.bfloat16)
    value_part = (projected[:, 2 * D :] + b_proj[D:]).astype(jnp.bfloat16)
    keys_all, values_all = (
        lax.all_gather(key_part, "band", axis=0, tiled=True),
        lax.all_gather(value_part, "band", axis=0, tiled=True),
    )
    seg_keys = jnp.tile(segment, parts)
    query_heads = split_heads(query, heads)
    keys_heads = split_heads(keys_all, heads)
    values_heads = split_heads(values_all, heads)
    head_out, log_total = attend_forward(
        query_heads, keys_heads, values_heads, segment, seg_keys, count
    )
    mixed = merge_heads(head_out).astype(jnp.bfloat16)
    hidden = value + (inner_dot(mixed, w_mix) + b_mix)
    normed_mid, pull_two = jax.vjp(normed, hidden, gain_two, shift_two)
    mid_low = normed_mid.astype(jnp.bfloat16)
    upward = inner_dot(mid_low, w_rise) + b_rise
    active, pull_gelu = jax.vjp(gelu_tanh, upward)
    active_low = active.astype(jnp.bfloat16)
    output = hidden + (inner_dot(active_low, w_fall) + b_fall)
    grad_y = cotangent.astype(jnp.float32) * (segment != 0).astype(jnp.float32)[:, None]
    grad_m = grad_y.astype(jnp.bfloat16)
    grad_w_fall = row_dot(active_low, grad_m)
    grad_b_fall = jnp.sum(grad_m.astype(jnp.float32), axis=0)
    grad_up = pull_gelu(col_dot(grad_m, w_fall))[0].astype(jnp.bfloat16)
    grad_w_rise = row_dot(mid_low, grad_up)
    grad_b_rise = jnp.sum(grad_up.astype(jnp.float32), axis=0)
    grad_mid, grad_gain_two, grad_shift_two = pull_two(col_dot(grad_up, w_rise))
    grad_hidden = grad_y + grad_mid
    grad_a = grad_hidden.astype(jnp.bfloat16)
    grad_w_mix = row_dot(mixed, grad_a)
    grad_b_mix = jnp.sum(grad_a.astype(jnp.float32), axis=0)
    grad_mixed = col_dot(grad_a, w_mix).astype(jnp.bfloat16)
    grad_heads = split_heads(grad_mixed, heads)
    grad_query, grad_keys, grad_values = attend_backward(
        query_heads, keys_heads, values_heads, grad_heads, log_total, segment, seg_keys, count
    )
    keys_sum, values_sum = (
        lax.psum_scatter(
            merge_heads(grad_keys).astype(jnp.bfloat16), "band", scatter_dimension=0, tiled=True
        ).astype(jnp.float32),
        lax.psum_scatter(
            merge_heads(grad_values).astype(jnp.bfloat16), "band", scatter_dimension=0, tiled=True
        ).astype(jnp.float32),
    )
    query_low = merge_heads(grad_query).astype(jnp.bfloat16)
    values_low = values_sum.astype(jnp.bfloat16)
    grad_qkv = jnp.concatenate([query_low, keys_sum.astype(jnp.bfloat16), values_low], axis=1)
    grad_w_proj = row_dot(normed_low, grad_qkv)
    grad_b_proj = jnp.concatenate(
        [
            jnp.sum(query_low.astype(jnp.float32), axis=0),
            jnp.sum(values_low.astype(jnp.float32), axis=0),
        ]
    )
    grad_norm_in, grad_gain_one, grad_shift_one = pull_one(col_dot(grad_qkv, w_proj))
    grad_input = grad_hidden + grad_norm_in
    grads = (
        grad_gain_one,
        grad_shift_one,
        grad_w_proj,
        grad_b_proj,
        grad_w_mix,
        grad_b_mix,
        grad_gain_two,
        grad_shift_two,
        grad_w_rise,
        grad_b_rise,
        grad_w_fall,
        grad_b_fall,
    )
    return (output.astype(jnp.bfloat16), grad_input.astype(jnp.bfloat16), grads)


def gather_each(shards):
    return (
        lax.all_gather(shards[0], "band", axis=0, tiled=True),
        lax.all_gather(shards[1], "band", axis=0, tiled=True),
        lax.all_gather(shards[2], "band", axis=0, tiled=True),
        lax.all_gather(shards[3], "band", axis=0, tiled=True),
        lax.all_gather(shards[4], "band", axis=0, tiled=True),
        lax.all_gather(shards[5], "band", axis=0, tiled=True),
        lax.all_gather(shards[6], "band", axis=0, tiled=True),
        lax.all_gather(shards[7], "band", axis=0, tiled=True),
        lax.all_gather(shards[8], "band", axis=0, tiled=True),
        lax.all_gather(shards[9], "band", axis=0, tiled=True),
        lax.all_gather(shards[10], "band", axis=0, tiled=True),
        lax.all_gather(shards[11], "band", axis=0, tiled=True),
    )


def reduce_end(grads):
    shares = (
        lax.psum_scatter(
            grads[0].astype(jnp.bfloat16), "band", scatter_dimension=0, tiled=True
        ).astype(jnp.float32),
        lax.psum_scatter(
            grads[1].astype(jnp.bfloat16), "band", scatter_dimension=0, tiled=True
        ).astype(jnp.float32),
        lax.psum_scatter(
            grads[2].astype(jnp.bfloat16), "band", scatter_dimension=0, tiled=True
        ).astype(jnp.float32),
        lax.psum_scatter(
            grads[3].astype(jnp.bfloat16), "band", scatter_dimension=0, tiled=True
        ).astype(jnp.float32),
        lax.psum_scatter(
            grads[4].astype(jnp.bfloat16), "band", scatter_dimension=0, tiled=True
        ).astype(jnp.float32),
        lax.psum_scatter(
            grads[5].astype(jnp.bfloat16), "band", scatter_dimension=0, tiled=True
        ).astype(jnp.float32),
        lax.psum_scatter(
            grads[6].astype(jnp.bfloat16), "band", scatter_dimension=0, tiled=True
        ).astype(jnp.float32),
        lax.psum_scatter(
            grads[7].astype(jnp.bfloat16), "band", scatter_dimension=0, tiled=True
        ).astype(jnp.float32),
        lax.psum_scatter(
            grads[8].astype(jnp.bfloat16), "band", scatter_dimension=0, tiled=True
        ).astype(jnp.float32),
        lax.psum_scatter(
            grads[9].astype(jnp.bfloat16), "band", scatter_dimension=0, tiled=True
        ).astype(jnp.float32),
        lax.psum_scatter(
            grads[10].astype(jnp.bfloat16), "band", scatter_dimension=0, tiled=True
        ).astype(jnp.float32),
        lax.psum_scatter(
            grads[11].astype(jnp.bfloat16), "band", scatter_dimension=0, tiled=True
        ).astype(jnp.float32),
    )
    return (
        lax.psum(shares[0].astype(jnp.bfloat16), "dp").astype(jnp.float32),
        lax.psum(shares[1].astype(jnp.bfloat16), "dp").astype(jnp.float32),
        lax.psum(shares[2].astype(jnp.bfloat16), "dp").astype(jnp.float32),
        lax.psum(shares[3].astype(jnp.bfloat16), "dp").astype(jnp.float32),
        lax.psum(shares[4].astype(jnp.bfloat16), "dp").astype(jnp.float32),
        lax.psum(shares[5].astype(jnp.bfloat16), "dp").astype(jnp.float32),
        lax.psum(shares[6].astype(jnp.bfloat16), "dp").astype(jnp.float32),
        lax.psum(shares[7].astype(jnp.bfloat16), "dp").astype(jnp.float32),
        lax.psum(shares[8].astype(jnp.bfloat16), "dp").astype(jnp.float32),
        lax.psum(shares[9].astype(jnp.bfloat16), "dp").astype(jnp.float32),
        lax.psum(shares[10].astype(jnp.bfloat16), "dp").astype(jnp.float32),
        lax.psum(shares[11].astype(jnp.bfloat16), "dp").astype(jnp.float32),
    )


def body(
    inputs,
    segments,
    cotangent,
    ln1_gain,
    ln1_bias,
    w_qkv,
    b_qv,
    w_out,
    b_out,
    ln2_gain,
    ln2_bias,
    w_up,
    b_up,
    w_down,
    b_down,
):
    shards = (
        ln1_gain,
        ln1_bias,
        w_qkv,
        b_qv,
        w_out,
        b_out,
        ln2_gain,
        ln2_bias,
        w_up,
        b_up,
        w_down,
        b_down,
    )
    parts = lax.axis_size("band")
    results = []
    grads_in = []
    totals = None
    for batch in range(inputs.shape[0]):
        whole = gather_each(shards)
        result, grad_in, grads = layer_pass(
            inputs[batch, 0], segments[batch, 0], cotangent[batch, 0], whole, parts
        )
        totals = (
            grads
            if totals is None
            else tuple((first + second for first, second in zip(totals, grads)))
        )
        results.append(result)
        grads_in.append(grad_in)
    totals = reduce_end(totals)
    return (jnp.stack(results)[:, None], jnp.stack(grads_in)[:, None]) + tuple(totals)


def solution(mesh):
    return jax.shard_map(
        body,
        mesh=mesh,
        in_specs=(
            P(None, "dp", "band", None),
            P(None, "dp", "band"),
            P(None, "dp", "band", None),
            P("band"),
            P("band"),
            P("band", None),
            P("band"),
            P("band", None),
            P("band"),
            P("band"),
            P("band"),
            P("band", None),
            P("band"),
            P("band", None),
            P("band"),
        ),
        out_specs=(
            P(None, "dp", "band", None),
            P(None, "dp", "band", None),
            P("band"),
            P("band"),
            P("band", None),
            P("band"),
            P("band", None),
            P("band"),
            P("band"),
            P("band"),
            P("band", None),
            P("band"),
            P("band", None),
            P("band"),
        ),
        check_vma=False,
    )
```

profile of v0, /device:TPU:0, one launch (start us, length us, event | category | flops | bytes accessed | tf_op | source)
XLA Modules:
  0.0 1097.5 jit_solution(7388853677042379467)
XLA Ops:
  14.2 13.5 %all-reduce.17 = (bf16[768]{0:T(1024)(128)(2,1)S(1)}, bf16[768]{0:T(1024)(128)(2,1)S(1)}, bf16[768]{0:T(1024)(128)(2,1)S(1)}, bf16[768]{0:T(1024)(128)(2,1)S(1)}, bf16[768]{0:T(1024)(128)(2,1)S(1)}) all-reduce(bf16[768]{0:T(1024)(128)(2,1)S(1)} %dynamic-update-slice.1, ...), channel_id=1, replica_groups=mesh['dp'=8,'band'=4] {'band'}, use_global_device_ids=true, to_apply=%add.1 | all-reduce | flops 3840 | bytes 15360
  28.3 5.3 all-gather
  36.6 6.6 all-gather.11.cloned.1.call-done
  43.2 4.3 fusion.162
  60.4 5.3 all-gather.1
  73.6 7.8 all-gather.25.cloned.1.call-done
  81.5 4.8 copy.71
  86.2 6.7 copy.74
  93.0 19.2 %all-gather.23.cloned.1.call-done = bf16[2048,768]{1,0:T(8,128)(2,1)} async-done(((bf16[512,768]{1,0:T(8,128)(2,1)}), bf16[2048,768]{1,0:T(8,128)(2,1)}) %all-gather.23.cloned.1.call-update) | async-done | bytes 3145744 | tf_op jit(solution)/shard_map/all_gather | solution.py:142
  112.2 4.7 copy.70
  116.9 6.7 copy.73
  124.6 104.7 %while.51 = (s32[]{:T(128)}, bf16[12,512,64]{1,2,0:T(8,128)(2,1)}, f32[12,512]{1,0:T(8,128)S(1)}, s32[1,1,512]{2,1,0:T(1,128)S(1)}, bf16[12,512,64]{2,1,0:T(8,12...) while((s32[]{:T(128)}, bf16[12,512,64]{1,2,0:T(8,128)(2,1)}, ...), condition=%wide.region_13.14_spmd.clone, body=%wide.region_10.13_spmd.clone.sunk | while | flops 277872128 | bytes 30730372 | solution.py:72
  181.3 3.9 fusion.255
  190.0 3.9 fusion.255
  198.7 4.4 fusion.255
  207.9 3.9 fusion.255
  216.6 4.0 fusion.255
  225.3 4.0 fusion.255
  229.3 5.3 copy.65
  234.6 6.7 copy.68
  241.3 4.8 copy.64
  246.1 6.6 copy.67
  252.7 97.4 %while.50 = (s32[]{:T(128)}, bf16[12,512,64]{1,2,0:T(8,128)(2,1)S(1)}, f32[12,512]{1,0:T(8,128)S(1)}, s32[1,1,512]{2,1,0:T(1,128)S(1)}, bf16[12,512,64]{2,1,0:T(...) while((s32[]{:T(128)}, ...), condition=%wide.region_5.6_spmd.clone, body=%wide.region_2.5_spmd.clone.sunk | while | flops 277872128 | bytes 30730372 | solution.py:72
  356.4 7.3 fusion.171
  363.7 5.0 fusion.170
  368.7 9.7 convert_reduce_fusion.1
  378.4 6.2 fusion.182
  385.1 8.8 convert_reduce_fusion
  408.1 130.6 %while.52 = (s32[]{:T(128)}, bf16[12,512,64]{1,2,0:T(8,128)(2,1)}, bf16[12,2048,64]{1,2,0:T(8,128)(2,1)S(1)}, bf16[12,2048,64]{1,2,0:T(8,128)(2,1)}, s32[1,1,512...) while((s32[]{:T(128)}, bf16[12,512,64]{1,2,0:T(8,128)(2,1)}, ...), condition=%wide.region_20.21_spmd.clone, body=%wide.region_18.20_spmd.clone.sunk | while | flops 681737728 | bytes 34655352 | solution.py:106
  538.7 4.3 convolution_convert_fusion
  548.8 139.4 %while.53 = (s32[]{:T(128)}, bf16[12,512,64]{1,2,0:T(8,128)(2,1)}, bf16[12,2048,64]{1,2,0:T(8,128)(2,1)S(1)}, bf16[12,2048,64]{1,2,0:T(8,128)(2,1)}, s32[1,1,512...) while((s32[]{:T(128)}, bf16[12,512,64]{1,2,0:T(8,128)(2,1)}, ...), condition=%wide.region_29.30_spmd.clone, body=%wide.region_27.29_spmd.clone.sunk | while | flops 681737728 | bytes 34655352 | solution.py:106
  694.0 6.4 fusion.150
  700.3 9.0 add_convert_fusion
  710.0 5.4 fusion.169
  715.4 4.9 add_convert_fusion.1
  721.7 6.9 fusion.135
  728.6 39.3 %reduce-scatter.15.cloned.1.call-done = bf16[512,768]{0,1:T(8,128)(2,1)} async-done(((bf16[2048,768]{0,1:T(8,128)(2,1)}), bf16[512,768]{0,1:T(8,128)(2,1)}) %reduce-scatter.15.cloned.1.call-update) | async-done | bytes 786448 | tf_op jit(solution)/shard_map/reduce_scatter | solution.py:181
  767.9 7.9 add_convert_fusion.2
  782.4 4.9 fusion.134
  787.4 4.4 fusion.121
  796.7 50.4 %reduce-scatter.23.cloned.1.call-done = bf16[768,768]{1,0:T(8,128)(2,1)} async-done(((bf16[3072,768]{1,0:T(8,128)(2,1)}), bf16[768,768]{1,0:T(8,128)(2,1)}) %reduce-scatter.23.cloned.1.call-update) | async-done | bytes 1179664 | tf_op jit(solution)/shard_map/reduce_scatter | solution.py:263
  847.1 50.4 %reduce-scatter.21.cloned.1.call-done = bf16[192,3072]{1,0:T(8,128)(2,1)} async-done(((bf16[768,3072]{1,0:T(8,128)(2,1)}), bf16[192,3072]{1,0:T(8,128)(2,1)}) %reduce-scatter.21.cloned.1.call-update) | async-done | bytes 1179664 | tf_op jit(solution)/shard_map/reduce_scatter | solution.py:257
  897.5 42.8 %reduce-scatter.17.cloned.1.call-done = bf16[192,2304]{1,0:T(8,128)(2,1)} async-done(((bf16[768,2304]{1,0:T(8,128)(2,1)}), bf16[192,2304]{1,0:T(8,128)(2,1)}) %reduce-scatter.17.cloned.1.call-update) | async-done | bytes 884752 | tf_op jit(solution)/shard_map/reduce_scatter | solution.py:239
  941.7 10.6 all-reduce.16
  952.8 23.1 %all-reduce.14 = (bf16[192]{0:T(256)(128)(2,1)S(1)}, bf16[192]{0:T(256)(128)(2,1)S(1)}, bf16[384]{0:T(512)(128)(2,1)S(1)}, bf16[192]{0:T(256)(128)(2,1)S(1)}, bf...) all-reduce(bf16[192]{0:T(256)(128)(2,1)S(1)} %dynamic-slice.7, ...), channel_id=1, replica_groups=mesh['dp'=8,'band'=4] {'dp'}, use_global_device_ids=true, to_apply=%region_37.38 | all-reduce | flops 2304 | bytes 9216 | tf_op jit(solution)/shard_map/psum | solution.py:271
  984.8 8.3 fusion.132
  993.1 8.3 fusion.133
  1002.7 81.0 %all-reduce.20.cloned.1.call-done = (bf16[192,2304]{1,0:T(8,128)(2,1)}, bf16[192,768]{1,0:T(8,128)(2,1)}, bf16[192,3072]{1,0:T(8,128)(2,1)}, bf16[768,768]{1,0:T(8,128)(2,1)}) async-done(((bf16[192,2304]{1,0:T(8,128)(2,1)}, bf16[192,768]{1,0:T(8,128)(2,1)}, bf16[192,3072]{1,0:T(8,128)(2,1)}, bf16[768,768]{1,0:T(8,128)(2,1)}), (bf16[192,2304]{1,0:T(8,128)(2,1)}, bf16[192,768]{1,0:T(8,128)(2,1)}, ...) | async-done | bytes 3538960 | tf_op jit(solution)/shard_map/psum | solution.py:273
  (749 shorter events, 540.1 us)
Async XLA Ops:
  7.2 28.2 %copy-start.2 = (bf16[2,1,512,768]{3,2,1,0:T(8,128)(2,1)S(1)}, bf16[2,1,512,768]{3,2,1,0:T(8,128)(2,1)}, u32[]{:S(2)}) copy-start(bf16[2,1,512,768]{3,2,1,0:T(8,128)(2,1)} %param.23) | copy-start | bytes 4718596
  7.2 36.0 %all-gather.11.cloned.1.call-start = ((), (), s32[]{:S(2)}) async-start(), calls=%async_computation.8 | async-start | bytes 4423680 | tf_op jit(solution)/shard_map/all_gather | solution.py:218
  7.9 73.6 %all-gather.25.cloned.1.call-start = ((), (), s32[]{:S(2)}) async-start(), calls=%async_computation.15 | async-start | bytes 3932160 | tf_op jit(solution)/shard_map/all_gather | solution.py:143
  27.6 19.9 %copy-start.37 = (f32[768]{0:T(1024)}, f32[768]{0:T(1024)S(1)}, u32[]{:S(2)}) copy-start(f32[768]{0:T(1024)S(1)} %convert_element_type.378) | copy-start | bytes 9220
  27.7 19.9 %copy-start.60 = (f32[768]{0:T(1024)}, f32[768]{0:T(1024)S(1)}, u32[]{:S(2)}) copy-start(f32[768]{0:T(1024)S(1)} %convert_element_type.379) | copy-start | bytes 9220
  35.4 12.2 %copy-start.40 = (f32[512]{0:T(512)}, f32[512]{0:T(512)S(1)}, u32[]{:S(2)}) copy-start(f32[512]{0:T(512)S(1)} %get-tuple-element.718) | copy-start | bytes 6148
  35.4 12.2 %copy-start.42 = (f32[512]{0:T(512)}, f32[512]{0:T(512)S(1)}, u32[]{:S(2)}) copy-start(f32[512]{0:T(512)S(1)} %get-tuple-element.719) | copy-start | bytes 6148
  36.6 11.0 copy-start.46
  36.6 11.0 copy-start.44
  52.7 59.5 %all-gather.23.cloned.1.call-start = ((), (), s32[]{:S(2)}) async-start(), calls=%async_computation.14 | async-start | bytes 3932160 | tf_op jit(solution)/shard_map/all_gather | solution.py:142
  55.1 174.1 %all-gather.15.cloned.1.call-start = ((), (), s32[]{:S(2)}) async-start(), calls=%async_computation.10 | async-start | bytes 3932160 | tf_op jit(solution)/shard_map/all_gather | solution.py:143
  55.8 185.6 %all-gather.13.cloned.1.call-start = ((), (), s32[]{:S(2)}) async-start(), calls=%async_computation.9 | async-start | bytes 3932160 | tf_op jit(solution)/shard_map/all_gather | solution.py:142
  58.2 291.9 %all-gather.17.cloned.1.call-start = ((), (), s32[]{:S(2)}) async-start(), calls=%async_computation.11 | async-start | bytes 1474560 | tf_op jit(solution)/shard_map/all_gather | solution.py:220
  58.8 297.5 %all-gather.19.cloned.1.call-start = ((), (), s32[]{:S(2)}) async-start(), calls=%async_computation.12 | async-start | bytes 5898240 | tf_op jit(solution)/shard_map/all_gather | solution.py:224
  59.5 309.1 %all-gather.21.cloned.1.call-start = ((), (), s32[]{:S(2)}) async-start(), calls=%async_computation.13 | async-start | bytes 5898240 | tf_op jit(solution)/shard_map/all_gather | solution.py:226
  60.3 660.3 %reduce-scatter.11.cloned.1.call-start = ((), (), s32[]{:S(2)}) async-start(), calls=%async_computation.17 | async-start | bytes 3932160 | tf_op jit(solution)/shard_map/reduce_scatter | solution.py:181
  60.4 303.2 %copy-start.62 = (f32[768]{0:T(1024)}, f32[768]{0:T(1024)S(1)}, u32[]{:S(2)}) copy-start(f32[768]{0:T(1024)S(1)} %convert_element_type.389) | copy-start | bytes 9220
  229.2 5.3 copy-start.20
  229.2 5.3 copy-start.34
  229.2 5.3 copy-start.39
  353.6 44.2 %copy-start.13 = (f32[512,768]{1,0:T(8,128)}, f32[512,768]{1,0:T(8,128)S(1)}, u32[]{:S(2)}) copy-start(f32[512,768]{1,0:T(8,128)S(1)} %get-tuple-element.709) | copy-start | bytes 4718596
  356.3 7.3 copy-start.17
  356.3 7.3 copy-start.71
  378.4 6.2 copy-start.79
  378.4 6.2 copy-start.70
  378.4 6.8 copy-start.78
  378.4 15.6 %slice-start = ((s8[4718592]{0:T(1024)(128)(4,1)}), s8[4194304]{0:T(1024)(128)(4,1)S(1)}, s32[]{:S(2)}) async-start(s8[4718592]{0:T(1024)(128)(4,1)} %bitcast.463), calls=%async_computation.25 | async-start | bytes 8388608
  385.1 8.8 copy-start.18
  385.1 8.8 slice-start.1
  538.7 182.0 %reduce-scatter.9.cloned.1.call-start = ((), (), s32[]{:S(2)}) async-start(), calls=%async_computation.16 | async-start | bytes 3932160 | tf_op jit(solution)/shard_map/reduce_scatter | solution.py:178
  545.4 183.3 %reduce-scatter.13.cloned.1.call-start = ((), (), s32[]{:S(2)}) async-start(), calls=%async_computation.18 | async-start | bytes 3932160 | tf_op jit(solution)/shard_map/reduce_scatter | solution.py:178
  689.9 78.0 %reduce-scatter.15.cloned.1.call-start = ((), (), s32[]{:S(2)}) async-start(), calls=%async_computation.19 | async-start | bytes 3932160 | tf_op jit(solution)/shard_map/reduce_scatter | solution.py:181
  690.5 106.2 %reduce-scatter.19.cloned.1.call-start = ((), (), s32[]{:S(2)}) async-start(), calls=%async_computation.21 | async-start | bytes 1474560 | tf_op jit(solution)/shard_map/reduce_scatter | solution.py:245
  693.9 153.2 %reduce-scatter.23.cloned.1.call-start = ((), (), s32[]{:S(2)}) async-start(), calls=%async_computation.23 | async-start | bytes 5898240 | tf_op jit(solution)/shard_map/reduce_scatter | solution.py:263
  709.4 6.0 copy-start.14
  709.4 188.1 %reduce-scatter.21.cloned.1.call-start = ((), (), s32[]{:S(2)}) async-start(), calls=%async_computation.22 | async-start | bytes 5898240 | tf_op jit(solution)/shard_map/reduce_scatter | solution.py:257
  710.0 5.4 copy-start.81
  720.3 219.9 %reduce-scatter.17.cloned.1.call-start = ((), (), s32[]{:S(2)}) async-start(), calls=%async_computation.20 | async-start | bytes 4423680 | tf_op jit(solution)/shard_map/reduce_scatter | solution.py:239
  721.7 46.2 %copy-start.41 = (f32[512]{0:T(512)S(1)}, f32[512]{0:T(512)}, u32[]{:S(2)}) copy-start(f32[512]{0:T(512)} %copy-done.40) | copy-start | bytes 6148
  721.7 46.2 %copy-start.45 = (f32[512]{0:T(512)S(1)}, f32[512]{0:T(512)}, u32[]{:S(2)}) copy-start(f32[512]{0:T(512)} %copy-done.44) | copy-start | bytes 6148
  775.8 5.2 copy-start.56
  775.8 5.2 copy-start.57
  775.8 5.2 copy-start.58
  775.8 5.2 copy-start.59
  775.9 307.9 %all-reduce.20.cloned.1.call-start = ((), (), s32[]{:S(2)}) async-start(), calls=%async_computation.24 | async-start | bytes 7077888 | tf_op jit(solution)/shard_map/psum | solution.py:273
  795.5 185.0 %copy-start.5 = (f32[512,768]{1,0:T(8,128)S(1)}, f32[512,768]{1,0:T(8,128)}, u32[]{:S(2)}) copy-start(f32[512,768]{1,0:T(8,128)} %copy-done.4) | copy-start | bytes 4718596
  795.5 185.0 %copy-start.49 = (f32[512]{0:T(512)S(1)}, f32[512]{0:T(512)}, u32[]{:S(2)}) copy-start(f32[512]{0:T(512)} %copy-done.48) | copy-start | bytes 6148
  984.8 8.3 copy-start.15
  (75 other events, 189.0 us)
Sparse Core Ops, SparseCore 0:
  9.6 33.6 all-gather.10
  52.8 28.6 all-gather.24
  83.6 28.4 all-gather.22
  114.2 28.5 all-gather.14
  144.1 28.5 all-gather.12
  174.1 17.4 all-gather.16
  193.1 37.4 all-gather.18
  232.1 37.4 all-gather.20
  538.8 37.8 reduce-scatter.10
  579.1 37.7 reduce-scatter.8
  690.0 37.7 reduce-scatter.12
  730.2 37.6 reduce-scatter.14
  771.1 25.6 reduce-scatter.18
  799.1 47.9 reduce-scatter.22
  849.5 47.9 reduce-scatter.20
  899.9 40.3 reduce-scatter.16
  944.1 139.5 all-reduce.19
where the time goes:
time: 1110 us; the launch traced here: 1100 us
  matrix products  508 us (46%)
  waiting for transfers between devices  303 us (27%)
  local copies, waits for them, and re-layouts  147 us (13%)
  other arithmetic  61.5 us (6%)
  blocking collectives  57.8 us (5%)
  between operations  18.2 us (2%)
    dot_general x80, matrix products, col_dot(): lax.dot_general(left, right, (((1,), (1,)), ((), ())), preferred_element_...  197 us
    dot_general x56, matrix products, inner_dot(): return jnp.dot(left, right, preferred_element_type=jnp.float32)  184 us
    dot_general x56, matrix products, row_dot(): lax.dot_general(left, right, (((0,), (0,)), ((), ())), preferred_element_...  127 us
    psum x1, waiting for transfers between devices, reduce_end(): lax.psum(shares[2].astype(jnp.bfloat16), 'dp').astype(jnp.float32)  81 us
    reduce_scatter x1, waiting for transfers between devices, reduce_end(): lax.psum_scatter(grads[10].astype(jnp.bfloat16), 'band', scatter_dimensio...  50.4 us
    reduce_scatter x1, waiting for transfers between devices, reduce_end(): lax.psum_scatter(grads[8].astype(jnp.bfloat16), 'band', scatter_dimension...  50.4 us
    while x144, local copies, waits for them, and re-layouts  49.5 us
    unnamed x193, local copies, waits for them, and re-layouts  47.7 us
  transfers between devices with their start and end apart: 17, of which 9 were waited for; matrix products, arithmetic and copies ran while one was open for 43% of the time, Pallas kernels for 0%

commit v1 on v0

v1 whole, which is shorter than its diff:
```python
import functools

import jax
import jax.numpy as jnp
from jax import lax
from jax.sharding import PartitionSpec as P
from jax.experimental import pallas as pl
from jax.experimental.pallas import tpu as pltpu
bf=jnp.bfloat16; f32=jnp.float32
HD=64
def nt(a,b): return lax.dot_general(a,b,(((1,),(1,)),((),())),preferred_element_type=f32)
def nn(a,b): return lax.dot_general(a,b,(((1,),(0,)),((),())),preferred_element_type=f32)
def tn(a,b): return lax.dot_general(a,b,(((0,),(0,)),((),())),preferred_element_type=f32)
def lanes(shape): return lax.broadcasted_iota(jnp.int32,shape,1)
NEG=-1e30

def mask_feats_q(seg, base):
    l=lanes((seg.shape[0],2*HD))
    return (l==seg+base).astype(f32)
def mask_feats_k(seg, base):
    l=lanes((seg.shape[0],2*HD))
    inr=(l>=base)&(l<base+8)
    return jnp.where(inr&(l!=seg+base),NEG,0.0)

def fwd_kernel(q_ref,k_ref,v_ref,segq_ref,segk_ref,o_ref,lse_ref,*,tq):
    n=q_ref.shape[0]
    k=k_ref[...]; v=v_ref[...]
    segk=segk_ref[...]
    lk=lanes(k.shape)<HD
    ks=[jnp.where(lk,k,mask_feats_k(segk,HD).astype(bf)),
        jnp.where(lk,mask_feats_k(segk,0).astype(bf),k)]
    for t in range(n//tq):
        rows=pl.ds(t*tq,tq)
        q=q_ref[rows,:]*jnp.asarray(0.125,bf)
        lq=lanes(q.shape)<HD
        segq=segq_ref[rows,:]
        outs=[];lses=[]
        for h in range(2):
            qq=jnp.where(lq,q,mask_feats_q(segq,HD).astype(bf)) if h==0 else jnp.where(lq,mask_feats_q(segq,0).astype(bf),q)
            s=nt(qq,ks[h])
            m=jnp.max(s,axis=-1,keepdims=True)
            p=jnp.exp(s-m)
            l=jnp.sum(p,axis=-1,keepdims=True)
            o=nn(p.astype(bf),v)
            outs.append(o/l); lses.append(m+jnp.log(l))
        o_ref[rows,:]=jnp.where(lq,outs[0],outs[1]).astype(bf)
        lse_ref[rows,:]=jnp.where(lq,jnp.broadcast_to(lses[0],q.shape),jnp.broadcast_to(lses[1],q.shape))

def attn_fwd(q,k,v,segq,segk,tq=256):
    n,d=q.shape; m=k.shape[0]
    pairs=d//(2*HD)
    col=lambda r: pl.BlockSpec((r,2*HD),lambda h:(0,h))
    full=lambda r: pl.BlockSpec((r,1),lambda h:(0,0))
    return pl.pallas_call(functools.partial(fwd_kernel,tq=tq),grid=(pairs,),
        in_specs=[col(n),col(m),col(m),full(n),full(m)],
        out_specs=[col(n),col(n)],
        out_shape=[jax.ShapeDtypeStruct((n,d),bf),jax.ShapeDtypeStruct((n,d),f32)],
        name="attn_fwd")(q,k,v,segq[:,None],segk[:,None])

def bwd_kernel(q_ref,k_ref,v_ref,do_ref,o_ref,lse_ref,segq_ref,segk_ref,dq_ref,dk_ref,dv_ref,*,tq,tk):
    n=q_ref.shape[0]; mkeys=k_ref.shape[0]
    for c in range(mkeys//tk):
        kr=pl.ds(c*tk,tk)
        k=k_ref[kr,:]; v=v_ref[kr,:]; segk=segk_ref[kr,:]
        lk=lanes(k.shape)<HD
        z=jnp.zeros_like(k)
        ks=[jnp.where(lk,k,mask_feats_k(segk,HD).astype(bf)), jnp.where(lk,mask_feats_k(segk,0).astype(bf),k)]
        km=[jnp.where(lk,k,z),jnp.where(lk,z,k)]
        dk=jnp.zeros((tk,2*HD),f32); dv=jnp.zeros((tk,2*HD),f32)
        for t in range(n//tq):
            rows=pl.ds(t*tq,tq)
            q=q_ref[rows,:]*jnp.asarray(0.125,bf); do=do_ref[rows,:]
            lq=lanes(q.shape)<HD
            zq=jnp.zeros_like(q)
            segq=segq_ref[rows,:]
            lse=lse_ref[rows,:]
            prod=do.astype(f32)*o_ref[rows,:].astype(f32)
            dqs=None
            for h in range(2):
                own=lq if h==0 else ~lq
                qq=jnp.where(own,q,mask_feats_q(segq,HD if h==0 else 0).astype(bf))
                qm=jnp.where(own,q,zq); dom=jnp.where(own,do,zq)
                dd=jnp.sum(jnp.where(own,prod,0.0),axis=-1,keepdims=True)
                ls=lse[:,:1] if h==0 else lse[:,HD:HD+1]
                p=jnp.exp(nt(qq,ks[h])-ls)
                dp=nt(dom,v)
                ds=(p*(dp-dd)).astype(bf)
                dv=dv+tn(p.astype(bf),dom)
                dk=dk+tn(ds,qm)
                x=nn(ds,km[h])
                dqs=x if dqs is None else dqs+x
            dqs=dqs*0.125
            if c==0: dq_ref[rows,:]=dqs
            else: dq_ref[rows,:]+=dqs
        dk_ref[kr,:]=dk.astype(bf); dv_ref[kr,:]=dv.astype(bf)

def attn_bwd(q,k,v,do,o,lse,segq,segk,tq=256,tk=1024):
    n,d=q.shape; m=k.shape[0]
    pairs=d//(2*HD)
    col=lambda r: pl.BlockSpec((r,2*HD),lambda h:(0,h))
    full=lambda r: pl.BlockSpec((r,1),lambda h:(0,0))
    return pl.pallas_call(functools.partial(bwd_kernel,tq=tq,tk=tk),grid=(pairs,),
        in_specs=[col(n),col(m),col(m),col(n),col(n),col(n),full(n),full(m)],
        out_specs=[col(n),col(m),col(m)],
        out_shape=[jax.ShapeDtypeStruct((n,d),f32),jax.ShapeDtypeStruct((m,d),bf),jax.ShapeDtypeStruct((m,d),bf)],
        name="attn_bwd")(q,k,v,do,o,lse,segq[:,None],segk[:,None])


def normed(value, gain, shift):
    center = value - jnp.mean(value, axis=-1, keepdims=True)
    spread = jnp.mean(center * center, axis=-1, keepdims=True)
    return center * lax.rsqrt(spread + 1e-06) * gain + shift


def gelu_tanh(value):
    return jax.nn.gelu(value, approximate=True)


def swap(x, flip):
    parts = lax.axis_size("band")
    return lax.ppermute(x, "band", [(i, i ^ flip) for i in range(parts)])


def gather_relative(x):
    flip = lax.axis_size("band") // 2
    while flip >= 1:
        x = jnp.concatenate([x, swap(x, flip)], axis=0)
        flip //= 2
    return x


def reduce_relative(x):
    flip = 1
    while flip < lax.axis_size("band"):
        half = x.shape[0] // 2
        x = (x[:half].astype(f32) + swap(x[half:], flip).astype(f32)).astype(bf)
        flip *= 2
    return x


VECTORS = ("ln1_gain", "ln1_bias", "b_qv", "b_out", "ln2_gain", "ln2_bias", "b_up", "b_down")


def gather_vectors(shards):
    parts = lax.axis_size("band")
    packed = jnp.concatenate(shards)
    whole = lax.all_gather(packed, "band", axis=0, tiled=False)
    out, at = [], 0
    for shard in shards:
        out.append(whole[:, at : at + shard.shape[0]].reshape(-1).astype(f32))
        at += shard.shape[0]
    return out


def reduce_vectors(grads, shards):
    parts = lax.axis_size("band")
    packed = jnp.concatenate([g.reshape(parts, -1) for g in grads], axis=1).astype(bf)
    total = lax.psum(packed, ("dp", "band"))
    mine = lax.dynamic_index_in_dim(total, lax.axis_index("band"), 0, keepdims=False).astype(f32)
    out, at = [], 0
    for shard in shards:
        out.append(mine[at : at + shard.shape[0]])
        at += shard.shape[0]
    return out


def gather_matrix(shard):
    return lax.all_gather(shard, "band", axis=0, tiled=True)


def reduce_matrix(grad):
    part = lax.psum_scatter(grad.astype(bf), "band", scatter_dimension=0, tiled=True)
    return lax.psum(part, "dp").astype(f32)


def body(inputs, segments, cotangent, ln1_gain, ln1_bias, w_qkv, b_qv, w_out, b_out, ln2_gain, ln2_bias, w_up, b_up, w_down, b_down):
    micro, tokens, width = inputs.shape[0], inputs.shape[2], inputs.shape[3]
    parts = lax.axis_size("band")
    vectors = (ln1_gain, ln1_bias, b_qv, b_out, ln2_gain, ln2_bias, b_up, b_down)
    gain_one, shift_one, bias_qv, bias_out, gain_two, shift_two, bias_up, bias_down = gather_vectors(vectors)
    w_proj = gather_matrix(w_qkv)
    w_mix = gather_matrix(w_out)
    w_rise = gather_matrix(w_up)
    w_fall = gather_matrix(w_down)

    value = inputs.reshape(micro * tokens, width).astype(f32)
    seg = segments.reshape(micro, tokens)
    normed_in, pull_one = jax.vjp(normed, value, gain_one, shift_one)
    normed_low = normed_in.astype(bf)
    projected = nn(normed_low, w_proj)
    query = (projected[:, :width] + bias_qv[:width]).astype(bf)
    keys = projected[:, width : 2 * width].astype(bf)
    values = (projected[:, 2 * width :] + bias_qv[width:]).astype(bf)

    saved, mixes = [], []
    for m in range(micro):
        rows = slice(m * tokens, (m + 1) * tokens)
        keys_all = gather_relative(keys[rows])
        values_all = gather_relative(values[rows])
        seg_keys = jnp.tile(seg[m], parts)
        mix, log_total = attn_fwd(query[rows], keys_all, values_all, seg[m], seg_keys)
        mixes.append(mix)
        saved.append((query[rows], keys_all, values_all, mix, log_total, seg[m], seg_keys))
    mixed = jnp.concatenate(mixes)

    hidden = value + (nn(mixed, w_mix) + bias_out)
    normed_mid, pull_two = jax.vjp(normed, hidden, gain_two, shift_two)
    mid_low = normed_mid.astype(bf)
    upward = nn(mid_low, w_rise) + bias_up
    active, pull_gelu = jax.vjp(gelu_tanh, upward)
    active_low = active.astype(bf)
    output = (hidden + (nn(active_low, w_fall) + bias_down)).astype(bf)

    real = (seg.reshape(-1, 1) != 0).astype(f32)
    grad_y = cotangent.reshape(micro * tokens, width).astype(f32) * real
    grad_m = grad_y.astype(bf)
    grad_w_fall = tn(active_low, grad_m)
    grad_b_fall = jnp.sum(grad_m.astype(f32), axis=0)
    grad_up = pull_gelu(nt(grad_m, w_fall))[0].astype(bf)
    grad_w_rise = tn(mid_low, grad_up)
    grad_b_rise = jnp.sum(grad_up.astype(f32), axis=0)
    grad_mid, grad_gain_two, grad_shift_two = pull_two(nt(grad_up, w_rise))
    grad_hidden = grad_y + grad_mid
    grad_a = grad_hidden.astype(bf)
    grad_w_mix = tn(mixed, grad_a)
    grad_b_mix = jnp.sum(grad_a.astype(f32), axis=0)
    grad_mixed = nt(grad_a, w_mix).astype(bf)

    pieces = []
    for m in range(micro):
        rows = slice(m * tokens, (m + 1) * tokens)
        q, k, v, mix, log_total, seg_q, seg_k = saved[m]
        grad_q, grad_k, grad_v = attn_bwd(q, k, v, grad_mixed[rows], mix, log_total, seg_q, seg_k)
        pieces.append(
            jnp.concatenate([grad_q.astype(bf), reduce_relative(grad_k), reduce_relative(grad_v)], axis=1)
        )
    grad_qkv = jnp.concatenate(pieces)
    grad_w_proj = tn(normed_low, grad_qkv)
    sums = jnp.sum(grad_qkv.astype(f32), axis=0)
    grad_b_proj = jnp.concatenate([sums[:width], sums[2 * width :]])
    grad_norm_in, grad_gain_one, grad_shift_one = pull_one(nt(grad_qkv, w_proj))
    input_grad = (grad_hidden + grad_norm_in).astype(bf)

    small = reduce_vectors(
        (grad_gain_one, grad_shift_one, grad_b_proj, grad_b_mix, grad_gain_two, grad_shift_two, grad_b_rise, grad_b_fall),
        vectors,
    )
    return (
        output.reshape(inputs.shape),
        input_grad.reshape(inputs.shape),
        small[0],
        small[1],
        reduce_matrix(grad_w_proj),
        small[2],
        reduce_matrix(grad_w_mix),
        small[3],
        small[4],
        small[5],
        reduce_matrix(grad_w_rise),
        small[6],
        reduce_matrix(grad_w_fall),
        small[7],
    )


def solution(mesh):
    split = P(None, "dp", "band", None)
    rows, vector = P("band", None), P("band")
    weights = (vector, vector, rows, vector, rows, vector, vector, vector, rows, vector, rows, vector)
    return jax.shard_map(
        body,
        mesh=mesh,
        in_specs=(split, P(None, "dp", "band"), split) + weights,
        out_specs=(split, split) + weights,
        check_vma=False,
    )
```

time: 1110 us -> 715 us (0.64)
  matrix products: 508 us -> 131 us
  Pallas kernels: 0 us -> 133 us
  local copies, waits for them, and re-layouts: 147 us -> 28.9 us
  waiting for transfers between devices: 303 us -> 290 us
  other arithmetic: 61.5 us -> 49.3 us
    dot_general x192 -> x12, matrix products: 508 us -> 131 us  [the longest x4 59.1 us: tn(): lax.dot_general(a, b, (((0,), (0,)), ((), ())), preferred_element_type=f32)]
    ppermute x0 -> x16, waiting for transfers between devices: none -> 160 us  [swap(): return lax.ppermute(x, 'band', [(i, i ^ flip) for i in range(parts)])]
    reduce_scatter x8 -> x4, waiting for transfers between devices: 184 us -> 24.5 us  [reduce_matrix(): lax.psum_scatter(grad.astype(bf), 'band', scatter_dimension=0, tiled=True)]
    pallas_call x0 -> x4, Pallas kernels: none -> 133 us  [the longest x2 83.2 us: attn_bwd(): pl.pallas_call(functools.partial(bwd_kernel, tq=tq, tk=tk), grid=(pairs,)...]
    while x144 -> x0, local copies, waits for them, and re-layouts: 49.5 us -> none
    unnamed x193 -> x138, local copies, waits for them, and re-layouts: 47.7 us -> 13.1 us
    reduce_sum x30 -> x5, other arithmetic: 26.2 us -> 1.93 us  [the longest x3 0.9 us: body(): sums = jnp.sum(grad_qkv.astype(f32), axis=0)]
    unnamed x2 -> x0, blocking collectives: 24.1 us -> none
  transfers between devices with their start and end apart: 17 -> 25, of which waited for: 9 -> 10; matrix products, arithmetic and copies ran while one was open for 43% -> 23% of each run, Pallas kernels for 0% -> 19%
where the time goes in v1:
time: 715 us; the launch traced here: 708 us
  waiting for transfers between devices  290 us (41%)
  Pallas kernels  133 us (19%)
  matrix products  131 us (18%)
  blocking collectives  50 us (7%)
  other arithmetic  49.3 us (7%)
  local copies, waits for them, and re-layouts  28.9 us (4%)
  between operations  15.3 us (2%)
  starting transfers between devices  10.1 us (1%)
    ppermute x16, waiting for transfers between devices, swap(): return lax.ppermute(x, 'band', [(i, i ^ flip) for i in range(parts)])  160 us
    pallas_call x2, Pallas kernels, attn_bwd(): pl.pallas_call(functools.partial(bwd_kernel, tq=tq, tk=tk), grid=(pairs,)...  83.2 us
    psum x1, waiting for transfers between devices, reduce_matrix(): return lax.psum(part, 'dp').astype(f32)  77.9 us
    dot_general x4, matrix products, tn(): lax.dot_general(a, b, (((0,), (0,)), ((), ())), preferred_element_type=f32)  59.1 us
    pallas_call x2, Pallas kernels, attn_fwd(): pl.pallas_call(functools.partial(fwd_kernel, tq=tq), grid=(pairs,), in_sp...  50.1 us
    psum x1, blocking collectives, reduce_vectors(): total = lax.psum(packed, ('dp', 'band'))  43.7 us
    dot_general x4, matrix products, nt(): lax.dot_general(a, b, (((1,), (1,)), ((), ())), preferred_element_type=f32)  37.7 us
    dot_general x4, matrix products, nn(): lax.dot_general(a, b, (((1,), (0,)), ((), ())), preferred_element_type=f32)  34.4 us
  transfers between devices with their start and end apart: 25, of which 10 were waited for; matrix products, arithmetic and copies ran while one was open for 23% of the time, Pallas kernels for 19%

profile of v1, /device:TPU:0, one launch (start us, length us, event | category | flops | bytes accessed | tf_op | source)
XLA Modules:
  0.0 707.9 jit_solution(3406176790784011126)
XLA Ops:
  10.3 6.2 all-gather.1
  18.8 24.3 %all-gather.7.cloned.1.call-done = bf16[768,2304]{1,0:T(8,128)(2,1)} async-done(((bf16[192,2304]{1,0:T(8,128)(2,1)}), bf16[768,2304]{1,0:T(8,128)(2,1)}) %all-gather.7.cloned.1.call-update) | async-done | bytes 3538960 | tf_op jit(solution)/shard_map/all_gather | solution.py:168
  43.2 5.8 fusion.40
  49.6 1.7 collective-permute-start
  51.3 1.8 fusion.7
  55.4 49.5 %collective-permute-done = bf16[512,768]{1,0:T(8,128)(2,1)S(1)} collective-permute-done((bf16[512,768]{1,0:T(8,128)(2,1)S(1)}, bf16[512,768]{1,0:T(8,128)(2,1)S(1)}, u32[]{:S(2)}, u32[]{:S(2)}) %collective-permute-start) | collective-permute-done | bytes 786464 | tf_op jit(solution)/shard_map/ppermute | solution.py:121
  106.2 28.8 %collective-permute-done.2 = bf16[512,768]{1,0:T(8,128)(2,1)S(1)} collective-permute-done((bf16[512,768]{1,0:T(8,128)(2,1)S(1)}, bf16[512,768]{1,0:T(8,128)(2,1)S(1)}, u32[]{:S(2)}, u32[]{:S(2)}) %collective-permute-start.2) | collective-permute-done | bytes 786464 | tf_op jit(solution)/shard_map/ppermute | solution.py:121
  138.2 19.7 %collective-permute-done.6 = bf16[512,768]{1,0:T(8,128)(2,1)S(1)} collective-permute-done((bf16[512,768]{1,0:T(8,128)(2,1)S(1)}, bf16[512,768]{1,0:T(8,128)(2,1)S(1)}, u32[]{:S(2)}, u32[]{:S(2)}) %collective-permute-start.6) | collective-permute-done | bytes 786464 | tf_op jit(solution)/shard_map/ppermute | solution.py:121
  167.3 3.4 pad_maximum_fusion.k_ref
  170.6 3.2 pad_maximum_fusion.1.v_ref
  173.9 25.2 %attn_fwd.2 = (bf16[512,768]{1,0:T(8,128)(2,1)}, f32[512,768]{1,0:T(8,128)}) custom-call(bf16[512,768]{1,0:T(8,128)(2,1)} %get-tuple-element.100.q_ref, bf16[2048,768]{1,0:T(8,128)(2,1)} %pad_maximum_fusion.k_ref, bf16[2048,768]{1,0:T(8,128)(2,1)} %pad_maximum_fusion.1.v_ref, s32[512,1]{1,0:T(8,128)} %copy.41.segq_ref, s32[2048,1]{1,0:T(8,128)} %bitcast.99), custom_call_target="tpu_custom_call" | custom-call | tf_op jit(solution)/shard_map/attn_fwd/pallas_call | solution.py:54
  199.1 3.8 pad_maximum_fusion.2.k_ref
  202.9 3.3 pad_maximum_fusion.3.v_ref
  206.2 24.9 %attn_fwd.3 = (bf16[512,768]{1,0:T(8,128)(2,1)}, f32[512,768]{1,0:T(8,128)}) custom-call(bf16[512,768]{1,0:T(8,128)(2,1)} %get-tuple-element.99.q_ref, bf16[2048,768]{1,0:T(8,128)(2,1)} %pad_maximum_fusion.2.k_ref, bf16[2048,768]{1,0:T(8,128)(2,1)} %pad_maximum_fusion.3.v_ref, s32[512,1]{1,0:T(8,128)} %copy.43.segq_ref, s32[2048,1]{1,0:T(8,128)} %bitcast.97), custom_call_target="tpu_custom_call" | custom-call | tf_op jit(solution)/shard_map/attn_fwd/pallas_call | solution.py:54
  231.1 2.1 constant_dynamic-update-slice_fusion.1
  233.1 2.1 constant_dynamic-update-slice_fusion
  235.2 3.3 fusion.41
  238.5 1.7 copy-done.3
  240.8 11.1 %fusion.27 = f32[1024,3072]{1,0:T(8,128)} fusion(bf16[768,3072]{1,0:T(8,128)(2,1)} %all-gather.11.cloned.1.call-done, f32[1024,768]{1,0:T(8,128)} %copy-done.3, f32[768]{0:T(1024)S(1)} %reshape.295, f32[768]{0:T(1024)S(1)} %reshape.294, f32[1024]{0:T(1024)S(1)} %fusion.23, f32[1024]{0:T(1024)S(1)} %broadcast_multiply_fusion), kind=kOutput, calls=%fused_computation.100 | convolution fusion | flops 4835770368 | bytes 20461568 | tf_op jit(solution)/shard_map/dot_general | solution.py:12
  251.9 16.5 %fusion.42 = (bf16[3072]{0:T(1024)(128)(2,1)S(1)}, bf16[1024,3072]{1,0:T(8,128)(2,1)S(1)}) fusion(f32[1024,3072]{1,0:T(8,128)} %fusion.27, f32[3072]{0:T(1024)S(1)} %reshape.296, bf16[1024,768]{1,0:T(8,128)(2,1)} %fusion.20, bf16[3072,768]{1,0:T(8,128)(2,1)} %all-gather.13.cloned.1.call-done), kind=kOutput, calls=%fused_computation.114 | convolution fusion | flops 4901041152 | bytes 25184256 | tf_op jit(solution)/shard_map/dot_general | solution.py:11
  268.5 5.7 multiply_reduce_fusion
  274.2 1.7 fusion.31
  278.6 3.9 convolution_convert_fusion.4
  282.6 10.5 %convolution_convert_fusion.1 = bf16[768,3072]{1,0:T(8,128)(2,1)} fusion(bf16[1024,3072]{1,0:T(8,128)(2,1)} %copy-done.62, f32[1024,768]{1,0:T(8,128)} %copy-done.3, f32[768]{0:T(1024)S(1)} %reshape.295, f32[768]{0:T(1024)S(1)} %reshape.294, f32[1024]{0:T(1024)S(1)} %fusion.23, f32[1024]{0:T(1024)S(1)} %broadcast_multiply_fusion), kind=kOutput, calls=%fused_computation.11 | convolution fusion | flops 4838129664 | bytes 14170112 | tf_op jit(solution)/shard_map/dot_general | solution.py:13
  293.2 12.6 %convolution_convert_fusion = bf16[3072,768]{1,0:T(8,128)(2,1)} fusion(bf16[1024,768]{1,0:T(8,128)(2,1)} %fusion.20, f32[1024,3072]{1,0:T(8,128)} %fusion.27, f32[3072]{0:T(1024)S(1)} %reshape.296), kind=kOutput, calls=%fused_computation.10 | convolution fusion | flops 4865654784 | bytes 18886656 | tf_op jit(solution)/shard_map/dot_general | solution.py:13
  305.8 3.2 convolution_convert_fusion.3
  310.2 41.7 %attn_bwd.2 = (f32[512,768]{1,0:T(8,128)}, bf16[2048,768]{1,0:T(8,128)(2,1)}, bf16[2048,768]{1,0:T(8,128)(2,1)}) custom-call(bf16[512,768]{1,0:T(8,128)(2,1)} %get-tuple-element.100.q_ref, bf16[2048,768]{1,0:T(8,128)(2,1)} %pad_maximum_fusion.k_ref, bf16[2048,768]{1,0:T(8,128)(2,1)} %pad_maximum_fusion.1.v_ref, bf16[512,768]{1,0:T(8,128)(2,1)} %get-tuple-element.95.do_ref, ...), custom_call_target="tpu_custom_call" | custom-call | tf_op jit(solution)/shard_map/attn_bwd/pallas_call | solution.py:102
  352.0 2.9 slice.236
  356.6 41.5 %attn_bwd.3 = (f32[512,768]{1,0:T(8,128)}, bf16[2048,768]{1,0:T(8,128)(2,1)}, bf16[2048,768]{1,0:T(8,128)(2,1)}) custom-call(bf16[512,768]{1,0:T(8,128)(2,1)} %get-tuple-element.99.q_ref, bf16[2048,768]{1,0:T(8,128)(2,1)} %pad_maximum_fusion.2.k_ref, bf16[2048,768]{1,0:T(8,128)(2,1)} %pad_maximum_fusion.3.v_ref, bf16[512,768]{1,0:T(8,128)(2,1)} %get-tuple-element.96.do_ref, ...), custom_call_target="tpu_custom_call" | custom-call | tf_op jit(solution)/shard_map/attn_bwd/pallas_call | solution.py:102
  398.1 1.7 slice.245
  403.0 2.0 add_convert_fusion.3
  405.4 2.1 add_convert_fusion.4
  407.5 1.6 collective-permute-start.9
  412.3 13.1 %collective-permute-done.11 = bf16[512,768]{1,0:T(8,128)(2,1)S(1)} collective-permute-done((bf16[512,768]{1,0:T(8,128)(2,1)S(1)}, bf16[512,768]{1,0:T(8,128)(2,1)S(1)}, u32[]{:S(2)}, u32[]{:S(2)}) %collective-permute-start.11) | collective-permute-done | bytes 786464 | tf_op jit(solution)/shard_map/ppermute | solution.py:121
  425.7 16.6 %collective-permute-done.9 = bf16[512,768]{1,0:T(8,128)(2,1)S(1)} collective-permute-done((bf16[512,768]{1,0:T(8,128)(2,1)S(1)}, bf16[512,768]{1,0:T(8,128)(2,1)S(1)}, u32[]{:S(2)}, u32[]{:S(2)}) %collective-permute-start.9) | collective-permute-done | bytes 786464 | tf_op jit(solution)/shard_map/ppermute | solution.py:121
  442.5 16.6 %collective-permute-done.15 = bf16[512,768]{1,0:T(8,128)(2,1)S(1)} collective-permute-done((bf16[512,768]{1,0:T(8,128)(2,1)S(1)}, bf16[512,768]{1,0:T(8,128)(2,1)S(1)}, u32[]{:S(2)}, u32[]{:S(2)}) %collective-permute-start.15) | collective-permute-done | bytes 786464 | tf_op jit(solution)/shard_map/ppermute | solution.py:121
  459.4 16.0 %collective-permute-done.13 = bf16[512,768]{1,0:T(8,128)(2,1)S(1)} collective-permute-done((bf16[512,768]{1,0:T(8,128)(2,1)S(1)}, bf16[512,768]{1,0:T(8,128)(2,1)S(1)}, u32[]{:S(2)}, u32[]{:S(2)}) %collective-permute-start.13) | collective-permute-done | bytes 786464 | tf_op jit(solution)/shard_map/ppermute | solution.py:121
  476.5 32.2 %convolution_convert_fusion.2 = bf16[768,2304]{1,0:T(8,128)(2,1)} fusion(bf16[1024,768]{1,0:T(8,128)(2,1)S(1)} %copy-done.38, bf16[512,768]{1,0:T(8,128)(2,1)S(1)} %add_convert_fusion.7, bf16[512,768]{1,0:T(8,128)(2,1)S(1)} %add_convert_fusion.8, bf16[512,768]{1,0:T(8,128)(2,1)S(1)} %convert_element_type.312, bf16[512,768]{1,0:T(8,128)(2,1)S(1)} %add_convert_fusion.9, ...), kind=kOutput, calls=%fused_computation.12 | convolution fusion | flops 3653959680 | bytes 9830400 | tf_op jit(solution)/shard_map/dot_general | solution.py:13
  509.6 14.2 %add_convert_fusion.5 = bf16[1024,768]{1,0:T(8,128)(2,1)} fusion(f32[1024,768]{1,0:T(8,128)} %copy-done.3, bf16[3072,768]{1,0:T(8,128)(2,1)} %all-gather.13.cloned.1.call-done, f32[768]{0:T(1024)S(1)} %reshape.297, f32[1024,3072]{1,0:T(8,128)} %fusion.27, f32[3072]{0:T(1024)S(1)} %reshape.296), kind=kOutput, calls=%fused_computation.49 | convolution fusion | flops 4865654784 | bytes 22035456 | tf_op jit(solution)/shard_map/dot_general | solution.py:12
  524.9 24.4 %reduce-scatter.5.cloned.1.call-done = bf16[192,2304]{1,0:T(8,128)(2,1)} async-done(((bf16[768,2304]{1,0:T(8,128)(2,1)}), bf16[192,2304]{1,0:T(8,128)(2,1)}) %reduce-scatter.5.cloned.1.call-update) | async-done | bytes 884752 | tf_op jit(solution)/shard_map/reduce_scatter | solution.py:172
  549.3 12.4 %fusion.28 = (bf16[768]{0:T(1024)(128)(2,1)S(1)}, f32[1024]{0:T(1024)S(1)}, f32[1024,768]{1,0:T(8,128)}) fusion(f32[768]{0:T(1024)S(1)} %copy-done.49, f32[1024]{0:T(1024)S(1)} %bitcast.109, bf16[2,1,512,768]{3,2,1,0:T(8,128)(2,1)S(1)} %copy-done, bf16[768,2304]{1,0:T(8,128)(2,1)} %all-gather.7.cloned.1.call-done, bf16[512,768]{1,0:T(8,128)(2,1)} %copy-done.33, ...), kind=kOutput, calls=%fused_computation.101 | convolution fusion | flops 3656907008 | bytes 12988928 | tf_op jit(solution)/shard_map/dot_general | solution.py:11
  561.8 3.0 fusion.16
  565.1 43.7 %psum.35 = bf16[4,2304]{1,0:T(4,128)(2,1)S(1)} all-reduce(bf16[4,2304]{1,0:T(4,128)(2,1)S(1)} %concatenate.66), channel_id=1, replica_groups=mesh['dp'=8,'band'=4] {'dp','band'}, use_global_device_ids=true, to_apply=%region_16.0 | all-reduce | flops 9216 | bytes 36864 | tf_op jit(solution)/shard_map/psum | solution.py:158
  610.7 4.5 add_convert_fusion
  615.3 77.9 %all-reduce.3.cloned.1.call-done = (bf16[192,2304]{1,0:T(8,128)(2,1)}, bf16[192,768]{1,0:T(8,128)(2,1)}, bf16[192,3072]{1,0:T(8,128)(2,1)}, bf16[768,768]{1,0:T(8,128)(2,1)}) async-done(((bf16[192,2304]{1,0:T(8,128)(2,1)}, bf16[192,768]{1,0:T(8,128)(2,1)}, bf16[192,3072]{1,0:T(8,128)(2,1)}, bf16[768,768]{1,0:T(8,128)(2,1)}), (bf16[192,2304]{1,0:T(8,128)(2,1)}, bf16[192,768]{1,0:T(8,128)(2,1)}, ...) | async-done | bytes 3538960 | tf_op jit(solution)/shard_map/psum | solution.py:173
  693.1 1.9 convert_element_type.338
  695.1 2.6 convert_element_type.336
  697.6 1.7 convert_element_type.340
  (259 shorter events, 42.5 us)
Async XLA Ops:
  7.3 35.9 %all-gather.7.cloned.1.call-start = ((), (), s32[]{:S(2)}) async-start(), calls=%async_computation.4 | async-start | bytes 4423680 | tf_op jit(solution)/shard_map/all_gather | solution.py:168
  8.0 227.2 %all-gather.9.cloned.1.call-start = ((), (), s32[]{:S(2)}) async-start(), calls=%async_computation.5 | async-start | bytes 1474560 | tf_op jit(solution)/shard_map/all_gather | solution.py:168
  8.8 232.0 %all-gather.11.cloned.1.call-start = ((), (), s32[]{:S(2)}) async-start(), calls=%async_computation.6 | async-start | bytes 5898240 | tf_op jit(solution)/shard_map/all_gather | solution.py:168
  9.5 242.4 %all-gather.13.cloned.1.call-start = ((), (), s32[]{:S(2)}) async-start(), calls=%async_computation.7 | async-start | bytes 5898240 | tf_op jit(solution)/shard_map/all_gather | solution.py:168
  10.1 514.7 %reduce-scatter.7.cloned.1.call-start = ((), (), s32[]{:S(2)}) async-start(), calls=%async_computation.9 | async-start | bytes 1474560 | tf_op jit(solution)/shard_map/reduce_scatter | solution.py:172
  16.9 32.1 %copy-start.44 = (f32[1,4,2,128]{3,1,2,0:T(4,128)}, f32[1,4,2,128]{3,1,2,0:T(4,128)S(1)}, u32[]{:S(2)}) copy-start(f32[1,4,2,128]{3,1,2,0:T(4,128)S(1)} %copy.53) | copy-start | bytes 12292
  17.6 31.4 %copy-start.46 = (f32[1024]{0:T(1024)}, f32[1024]{0:T(1024)S(1)}, u32[]{:S(2)}) copy-start(f32[1024]{0:T(1024)S(1)} %rsqrt.20) | copy-start | bytes 12292
  17.7 31.3 %copy-start.48 = (f32[768]{0:T(1024)}, f32[768]{0:T(1024)S(1)}, u32[]{:S(2)}) copy-start(f32[768]{0:T(1024)S(1)} %reshape.291) | copy-start | bytes 9220
  18.8 30.2 %copy-start.37 = (bf16[1024,768]{1,0:T(8,128)(2,1)}, bf16[1024,768]{1,0:T(8,128)(2,1)S(1)}, u32[]{:S(2)}) copy-start(bf16[1024,768]{1,0:T(8,128)(2,1)S(1)} %fusion.15) | copy-start | bytes 4718596
  49.2 55.7 %copy-start.8 = (bf16[512,768]{1,0:T(8,128)(2,1)}, bf16[512,768]{1,0:T(8,128)(2,1)S(1)}, u32[]{:S(2)}) copy-start(bf16[512,768]{1,0:T(8,128)(2,1)S(1)} %get-tuple-element.94) | copy-start | bytes 2359300
  49.2 87.1 %copy-start.5 = (bf16[512,768]{1,0:T(8,128)(2,1)}, bf16[512,768]{1,0:T(8,128)(2,1)S(1)}, u32[]{:S(2)}) copy-start(bf16[512,768]{1,0:T(8,128)(2,1)S(1)} %get-tuple-element.93) | copy-start | bytes 2359300
  49.2 87.1 %collective-permute-start.4 = (bf16[512,768]{1,0:T(8,128)(2,1)S(1)}, bf16[512,768]{1,0:T(8,128)(2,1)S(1)}, u32[]{:S(2)}, u32[]{:S(2)}) collective-permute-start(bf16[512,768]{1,0:T(8,128)(2,1)S(1)} %get-tuple-element.93), channel_id=1, source_target_pairs={{0,2},{1,3},{2,0},{3,1},{4,6},{5,7},{6,4},{7,5},{8,10},{9,11},{10,... | collective-permute-start | bytes 2359304 | tf_op jit(solution)/shard_map/ppermute | solution.py:121
  49.6 55.3 %collective-permute-start = (bf16[512,768]{1,0:T(8,128)(2,1)S(1)}, bf16[512,768]{1,0:T(8,128)(2,1)S(1)}, u32[]{:S(2)}, u32[]{:S(2)}) collective-permute-start(bf16[512,768]{1,0:T(8,128)(2,1)S(1)} %get-tuple-element.94), channel_id=1, source_target_pairs={{0,2},{1,3},{2,0},{3,1},{4,6},{5,7},{6,4},{7,5},{8,10},{9,11},{10,... | collective-permute-start | bytes 2359304 | tf_op jit(solution)/shard_map/ppermute | solution.py:121
  53.2 83.1 %copy-start.10 = (bf16[512,768]{1,0:T(8,128)(2,1)}, bf16[512,768]{1,0:T(8,128)(2,1)S(1)}, u32[]{:S(2)}) copy-start(bf16[512,768]{1,0:T(8,128)(2,1)S(1)} %get-tuple-element.98) | copy-start | bytes 2359300
  53.2 104.7 %copy-start.6 = (bf16[512,768]{1,0:T(8,128)(2,1)}, bf16[512,768]{1,0:T(8,128)(2,1)S(1)}, u32[]{:S(2)}) copy-start(bf16[512,768]{1,0:T(8,128)(2,1)S(1)} %get-tuple-element.97) | copy-start | bytes 2359300
  53.2 81.8 %collective-permute-start.2 = (bf16[512,768]{1,0:T(8,128)(2,1)S(1)}, bf16[512,768]{1,0:T(8,128)(2,1)S(1)}, u32[]{:S(2)}, u32[]{:S(2)}) collective-permute-start(bf16[512,768]{1,0:T(8,128)(2,1)S(1)} %get-tuple-element.98), channel_id=1, source_target_pairs={{0,2},{1,3},{2,0},{3,1},{4,6},{5,7},{6,4},{7,5},{8,10},{9,11},{10,... | collective-permute-start | bytes 2359304 | tf_op jit(solution)/shard_map/ppermute | solution.py:121
  53.8 104.0 %collective-permute-start.6 = (bf16[512,768]{1,0:T(8,128)(2,1)S(1)}, bf16[512,768]{1,0:T(8,128)(2,1)S(1)}, u32[]{:S(2)}, u32[]{:S(2)}) collective-permute-start(bf16[512,768]{1,0:T(8,128)(2,1)S(1)} %get-tuple-element.97), channel_id=1, source_target_pairs={{0,2},{1,3},{2,0},{3,1},{4,6},{5,7},{6,4},{7,5},{8,10},{9,11},{10,... | collective-permute-start | bytes 2359304 | tf_op jit(solution)/shard_map/ppermute | solution.py:121
  104.9 31.4 %copy-start.14 = (bf16[512,768]{1,0:T(8,128)(2,1)}, bf16[512,768]{1,0:T(8,128)(2,1)S(1)}, u32[]{:S(2)}) copy-start(bf16[512,768]{1,0:T(8,128)(2,1)S(1)} %collective-permute-done) | copy-start | bytes 2359300
  106.2 61.0 %collective-permute-start.1 = (bf16[1024,768]{1,0:T(8,128)(2,1)}, bf16[1024,768]{1,0:T(8,128)(2,1)}, u32[]{:S(2)}, u32[]{:S(2)}) collective-permute-start(bf16[1024,768]{1,0:T(8,128)(2,1)} %pad_maximum_fusion.4), channel_id=1, source_target_pairs={{0,1},{1,0},{2,3},{3,2},{4,5},{5,4},{6,7},{7,6},{8,9},{9,8},{10,11... | collective-permute-start | bytes 4718600 | tf_op jit(solution)/shard_map/ppermute | solution.py:121
  136.3 34.3 %collective-permute-start.3 = (bf16[1024,768]{1,0:T(8,128)(2,1)}, bf16[1024,768]{1,0:T(8,128)(2,1)}, u32[]{:S(2)}, u32[]{:S(2)}) collective-permute-start(bf16[1024,768]{1,0:T(8,128)(2,1)} %pad_maximum_fusion.5), channel_id=1, source_target_pairs={{0,1},{1,0},{2,3},{3,2},{4,5},{5,4},{6,7},{7,6},{8,9},{9,8},{10,11... | collective-permute-start | bytes 4718600 | tf_op jit(solution)/shard_map/ppermute | solution.py:121
  136.3 22.9 %copy-start.13 = (bf16[512,768]{1,0:T(8,128)(2,1)}, bf16[512,768]{1,0:T(8,128)(2,1)S(1)}, u32[]{:S(2)}) copy-start(bf16[512,768]{1,0:T(8,128)(2,1)S(1)} %collective-permute-done.4) | copy-start | bytes 2359300
  137.7 26.4 %copy-start.2 = (bf16[2,1,512,768]{3,2,1,0:T(8,128)(2,1)S(1)}, bf16[2,1,512,768]{3,2,1,0:T(8,128)(2,1)}, u32[]{:S(2)}) copy-start(bf16[2,1,512,768]{3,2,1,0:T(8,128)(2,1)} %param.17) | copy-start | bytes 4718596
  137.7 61.4 %collective-permute-start.5 = (bf16[1024,768]{1,0:T(8,128)(2,1)}, bf16[1024,768]{1,0:T(8,128)(2,1)}, u32[]{:S(2)}, u32[]{:S(2)}) collective-permute-start(bf16[1024,768]{1,0:T(8,128)(2,1)} %pad_maximum_fusion.6), channel_id=1, source_target_pairs={{0,1},{1,0},{2,3},{3,2},{4,5},{5,4},{6,7},{7,6},{8,9},{9,8},{10,11... | collective-permute-start | bytes 4718600 | tf_op jit(solution)/shard_map/ppermute | solution.py:121
  159.2 43.7 %collective-permute-start.7 = (bf16[1024,768]{1,0:T(8,128)(2,1)}, bf16[1024,768]{1,0:T(8,128)(2,1)}, u32[]{:S(2)}, u32[]{:S(2)}) collective-permute-start(bf16[1024,768]{1,0:T(8,128)(2,1)} %pad_maximum_fusion.7), channel_id=1, source_target_pairs={{0,1},{1,0},{2,3},{3,2},{4,5},{5,4},{6,7},{7,6},{8,9},{9,8},{10,11... | collective-permute-start | bytes 4718600 | tf_op jit(solution)/shard_map/ppermute | solution.py:121
  251.9 16.6 %copy-start.4 = (f32[1024,768]{1,0:T(8,128)S(1)}, f32[1024,768]{1,0:T(8,128)}, u32[]{:S(2)}) copy-start(f32[1024,768]{1,0:T(8,128)} %copy-done.3) | copy-start | bytes 9437188
  251.9 16.6 %copy-start.61 = (bf16[768,3072]{1,0:T(8,128)(2,1)S(1)}, bf16[768,3072]{1,0:T(8,128)(2,1)}, u32[]{:S(2)}) copy-start(bf16[768,3072]{1,0:T(8,128)(2,1)} %all-gather.11.cloned.1.call-done) | copy-start | bytes 14155780
  282.6 242.3 %reduce-scatter.9.cloned.1.call-start = ((), (), s32[]{:S(2)}) async-start(), calls=%async_computation.10 | async-start | bytes 5898240 | tf_op jit(solution)/shard_map/reduce_scatter | solution.py:172
  293.1 231.8 %reduce-scatter.11.cloned.1.call-start = ((), (), s32[]{:S(2)}) async-start(), calls=%async_computation.11 | async-start | bytes 5898240 | tf_op jit(solution)/shard_map/reduce_scatter | solution.py:172
  305.8 243.5 %reduce-scatter.5.cloned.1.call-start = ((), (), s32[]{:S(2)}) async-start(), calls=%async_computation.8 | async-start | bytes 4423680 | tf_op jit(solution)/shard_map/reduce_scatter | solution.py:172
  354.8 46.9 %collective-permute-start.10 = (bf16[1024,768]{1,0:T(8,128)(2,1)}, bf16[1024,768]{1,0:T(8,128)(2,1)}, u32[]{:S(2)}, u32[]{:S(2)}) collective-permute-start(bf16[1024,768]{1,0:T(8,128)(2,1)} %slice.236), channel_id=1, source_target_pairs={{0,1},{1,0},{2,3},{3,2},{4,5},{5,4},{6,7},{7,6},{8,9},{9,8},{10,11... | collective-permute-start | bytes 4718600 | tf_op jit(solution)/shard_map/ppermute | solution.py:121
  356.2 49.1 %collective-permute-start.8 = (bf16[1024,768]{1,0:T(8,128)(2,1)}, bf16[1024,768]{1,0:T(8,128)(2,1)}, u32[]{:S(2)}, u32[]{:S(2)}) collective-permute-start(bf16[1024,768]{1,0:T(8,128)(2,1)} %slice.232), channel_id=1, source_target_pairs={{0,1},{1,0},{2,3},{3,2},{4,5},{5,4},{6,7},{7,6},{8,9},{9,8},{10,11... | collective-permute-start | bytes 4718600 | tf_op jit(solution)/shard_map/ppermute | solution.py:121
  399.8 9.3 %collective-permute-start.14 = (bf16[1024,768]{1,0:T(8,128)(2,1)S(1)}, bf16[1024,768]{1,0:T(8,128)(2,1)S(1)}, u32[]{:S(2)}, u32[]{:S(2)}) collective-permute-start(bf16[1024,768]{1,0:T(8,128)(2,1)S(1)} %slice.245), channel_id=1, source_target_pairs={{0,1},{1,0},{2,3},{3,2},{4,5},{5,4},{6,7},{7,6},{8,9},{9,8},{10,11... | collective-permute-start | bytes 4718600 | tf_op jit(solution)/shard_map/ppermute | solution.py:121
  400.6 9.6 %collective-permute-start.12 = (bf16[1024,768]{1,0:T(8,128)(2,1)S(1)}, bf16[1024,768]{1,0:T(8,128)(2,1)S(1)}, u32[]{:S(2)}, u32[]{:S(2)}) collective-permute-start(bf16[1024,768]{1,0:T(8,128)(2,1)S(1)} %slice.241), channel_id=1, source_target_pairs={{0,1},{1,0},{2,3},{3,2},{4,5},{5,4},{6,7},{7,6},{8,9},{9,8},{10,11... | collective-permute-start | bytes 4718600 | tf_op jit(solution)/shard_map/ppermute | solution.py:121
  401.0 74.6 %copy-start.25 = (bf16[512,768]{1,0:T(8,128)(2,1)}, bf16[512,768]{1,0:T(8,128)(2,1)S(1)}, u32[]{:S(2)}) copy-start(bf16[512,768]{1,0:T(8,128)(2,1)S(1)} %convert_element_type.299) | copy-start | bytes 2359300
  401.7 73.9 %copy-start.27 = (bf16[512,768]{1,0:T(8,128)(2,1)}, bf16[512,768]{1,0:T(8,128)(2,1)S(1)}, u32[]{:S(2)}) copy-start(bf16[512,768]{1,0:T(8,128)(2,1)S(1)} %convert_element_type.312) | copy-start | bytes 2359300
  405.0 20.5 %collective-permute-start.11 = (bf16[512,768]{1,0:T(8,128)(2,1)S(1)}, bf16[512,768]{1,0:T(8,128)(2,1)S(1)}, u32[]{:S(2)}, u32[]{:S(2)}) collective-permute-start(bf16[512,768]{1,0:T(8,128)(2,1)S(1)} %slice.290), channel_id=1, source_target_pairs={{0,2},{1,3},{2,0},{3,1},{4,6},{5,7},{6,4},{7,5},{8,10},{9,11},{10,... | collective-permute-start | bytes 2359304 | tf_op jit(solution)/shard_map/ppermute | solution.py:121
  407.5 34.9 %collective-permute-start.9 = (bf16[512,768]{1,0:T(8,128)(2,1)S(1)}, bf16[512,768]{1,0:T(8,128)(2,1)S(1)}, u32[]{:S(2)}, u32[]{:S(2)}) collective-permute-start(bf16[512,768]{1,0:T(8,128)(2,1)S(1)} %slice.288), channel_id=1, source_target_pairs={{0,2},{1,3},{2,0},{3,1},{4,6},{5,7},{6,4},{7,5},{8,10},{9,11},{10,... | collective-permute-start | bytes 2359304 | tf_op jit(solution)/shard_map/ppermute | solution.py:121
  409.6 49.5 %collective-permute-start.15 = (bf16[512,768]{1,0:T(8,128)(2,1)S(1)}, bf16[512,768]{1,0:T(8,128)(2,1)S(1)}, u32[]{:S(2)}, u32[]{:S(2)}) collective-permute-start(bf16[512,768]{1,0:T(8,128)(2,1)S(1)} %slice.295), channel_id=1, source_target_pairs={{0,2},{1,3},{2,0},{3,1},{4,6},{5,7},{6,4},{7,5},{8,10},{9,11},{10,... | collective-permute-start | bytes 2359304 | tf_op jit(solution)/shard_map/ppermute | solution.py:121
  410.7 64.7 %collective-permute-start.13 = (bf16[512,768]{1,0:T(8,128)(2,1)S(1)}, bf16[512,768]{1,0:T(8,128)(2,1)S(1)}, u32[]{:S(2)}, u32[]{:S(2)}) collective-permute-start(bf16[512,768]{1,0:T(8,128)(2,1)S(1)} %slice.293), channel_id=1, source_target_pairs={{0,2},{1,3},{2,0},{3,1},{4,6},{5,7},{6,4},{7,5},{8,10},{9,11},{10,... | collective-permute-start | bytes 2359304 | tf_op jit(solution)/shard_map/ppermute | solution.py:121
  425.7 49.9 %copy-start.29 = (bf16[512,768]{1,0:T(8,128)(2,1)}, bf16[512,768]{1,0:T(8,128)(2,1)S(1)}, u32[]{:S(2)}) copy-start(bf16[512,768]{1,0:T(8,128)(2,1)S(1)} %add_convert_fusion.9) | copy-start | bytes 2359300
  425.7 50.8 %copy-start.38 = (bf16[1024,768]{1,0:T(8,128)(2,1)S(1)}, bf16[1024,768]{1,0:T(8,128)(2,1)}, u32[]{:S(2)}) copy-start(bf16[1024,768]{1,0:T(8,128)(2,1)} %copy-done.37) | copy-start | bytes 4718596
  442.5 33.1 %copy-start.31 = (bf16[512,768]{1,0:T(8,128)(2,1)}, bf16[512,768]{1,0:T(8,128)(2,1)S(1)}, u32[]{:S(2)}) copy-start(bf16[512,768]{1,0:T(8,128)(2,1)S(1)} %add_convert_fusion.10) | copy-start | bytes 2359300
  459.4 16.2 %copy-start.33 = (bf16[512,768]{1,0:T(8,128)(2,1)}, bf16[512,768]{1,0:T(8,128)(2,1)S(1)}, u32[]{:S(2)}) copy-start(bf16[512,768]{1,0:T(8,128)(2,1)S(1)} %add_convert_fusion.7) | copy-start | bytes 2359300
  508.7 184.4 %all-reduce.3.cloned.1.call-start = ((), (), s32[]{:S(2)}) async-start(), calls=%async_computation.12 | async-start | bytes 7077888 | tf_op jit(solution)/shard_map/psum | solution.py:173
  509.6 14.7 %copy-start.28 = (bf16[512,768]{1,0:T(8,128)(2,1)S(1)}, bf16[512,768]{1,0:T(8,128)(2,1)}, u32[]{:S(2)}) copy-start(bf16[512,768]{1,0:T(8,128)(2,1)} %copy-done.27) | copy-start | bytes 2359300
  509.6 14.7 %copy-start.34 = (bf16[512,768]{1,0:T(8,128)(2,1)S(1)}, bf16[512,768]{1,0:T(8,128)(2,1)}, u32[]{:S(2)}) copy-start(bf16[512,768]{1,0:T(8,128)(2,1)} %copy-done.33) | copy-start | bytes 2359300
  524.3 25.0 %copy-start.45 = (f32[1,4,2,128]{3,1,2,0:T(4,128)S(1)}, f32[1,4,2,128]{3,1,2,0:T(4,128)}, u32[]{:S(2)}) copy-start(f32[1,4,2,128]{3,1,2,0:T(4,128)} %copy-done.44) | copy-start | bytes 12292
  524.3 25.0 %copy-start.49 = (f32[768]{0:T(1024)S(1)}, f32[768]{0:T(1024)}, u32[]{:S(2)}) copy-start(f32[768]{0:T(1024)} %copy-done.48) | copy-start | bytes 9220
  (40 other events, 183.2 us)
Sparse Core Ops, SparseCore 0:
  9.6 33.4 all-gather.6
  44.7 23.8 all-gather.8
  70.2 62.8 all-gather.10
  134.5 43.5 all-gather.12
  282.7 25.6 reduce-scatter.6
  310.7 47.9 reduce-scatter.8
  361.3 47.9 reduce-scatter.10
  508.8 40.3 reduce-scatter.4
  553.2 139.8 all-reduce.2
